TPU v7x, 32 devices: a whole 2x2x4 slice. The times are simulated.
32 devices in a mesh: gx: 4 (over x, core), gy: 8 (over z, y).
Axes of the slice: x: 2, y: 2, z: 4, core: 2. Of those that a mesh axis runs over, the one named last changes fastest.
Arguments:
- snapshots: bfloat16 [2, 8192, 8192], P(None, 'gx', 'gy'), may hold values from -200 to 200
- mode_one_test: bfloat16 [2, 8192, 128], P(None, 'gy'), may hold values from -0.148231765 to 0.148231765
- mode_two_test: bfloat16 [2, 8192, 128], P(None, 'gx'), may hold values from -0.046875 to 0.046875
- row_sketch: bfloat16 [256, 8192], P(None, 'gx'), may hold values from -0.0625 to 0.0625
- column_sketch: bfloat16 [256, 8192], P(None, 'gy'), may hold values from -0.0625 to 0.0625
- old_mode_one: float32 [8192, 128], P('gx'), may hold values from -3 to 3
- old_mode_two: float32 [8192, 128], P('gy'), may hold values from -3 to 3
- old_core: float32 [9, 256, 256], replicated, may hold values from -3 to 3
- time_mix: float32 [9, 2], replicated, may hold values from -2.5 to 2.5
Outputs:
- basis: float32 [8192, 128], P(('gx', 'gy'))
- mode_two: float32 [8192, 128], P('gy')
- projected: float32 [128, 2, 8192], P('gx', None, 'gy')
- core: float32 [9, 256, 256], replicated
All inputs are finite; a program needn't handle non-finite values.
Results may differ from a plain program's by a relative error of at most 0.0024.
Values may be sent and summed in bfloat16 or wider, within the bound.
No kernel may reach another device: no remote copies, remote signals or barrier semaphores. Data moves between devices by JAX's collectives and lax.ppermute only.
A program may use at most 128 MiB of HBM per device.

v0:
```python
import math
import jax
import jax.numpy as jnp
from jax import lax
from jax.sharding import PartitionSpec as P


def orthonormal(sketch_rows, gram_matrix, root_rows):
    factor = jnp.linalg.cholesky(gram_matrix)
    return root_rows * jax.scipy.linalg.solve_triangular(factor, sketch_rows.T, lower=True).T


def body(
    snapshots,
    mode_one_test,
    mode_two_test,
    row_sketch,
    column_sketch,
    old_mode_one,
    old_mode_two,
    old_core,
    time_mix,
):
    tile_rows = snapshots.shape[1]
    root_rows = math.sqrt(tile_rows * lax.axis_size("gx"))
    part_two = jnp.einsum(
        "trc,trk->ck", snapshots, mode_two_test, preferred_element_type=jnp.float32
    )
    mode_two = old_mode_two + lax.psum(part_two, "gx")
    part_one = jnp.einsum(
        "trc,tck->rk", snapshots, mode_one_test, preferred_element_type=jnp.float32
    )
    folded = jnp.einsum("sr,trc->tsc", row_sketch, snapshots, preferred_element_type=jnp.float32)
    core_part = jnp.einsum(
        "tsc,uc->tsu", folded, column_sketch.astype(jnp.float32), precision=lax.Precision.HIGHEST
    )
    core_part = jnp.einsum("jt,tsu->jsu", time_mix, core_part, precision=lax.Precision.HIGHEST)
    core = old_core + lax.psum(core_part, ("gx", "gy"))
    row_share = tile_rows // lax.axis_size("gy")
    first_row = lax.axis_index("gy") * row_share
    whole_rows = lax.psum(part_one, "gy") + old_mode_one
    gram_matrix = lax.psum(jnp.dot(whole_rows.T, whole_rows, precision=lax.Precision.HIGHEST), "gx")
    full_basis = orthonormal(whole_rows, gram_matrix, root_rows)
    projected_part = jnp.einsum(
        "rk,trc->ktc",
        full_basis.astype(jnp.bfloat16),
        snapshots,
        preferred_element_type=jnp.float32,
    )
    basis_out = lax.dynamic_slice_in_dim(full_basis, first_row, row_share, 0)
    projected = lax.psum_scatter(projected_part, "gx", scatter_dimension=0, tiled=True) / root_rows
    return (basis_out, mode_two, projected, core)


def solution(mesh):
    placed = (
        P(None, "gx", "gy"),
        P(None, "gy", None),
        P(None, "gx", None),
        P(None, "gx"),
        P(None, "gy"),
        P("gx", None),
        P("gy", None),
        P(),
        P(),
    )
    return jax.shard_map(
        body,
        mesh=mesh,
        in_specs=placed,
        out_specs=(P(("gx", "gy"), None), P("gy", None), P("gx", None, "gy"), P()),
        check_vma=False,
    )
```

profile of v0, /device:TPU:0, one launch (start us, length us, event | category | flops | bytes accessed | tf_op | source)
XLA Modules:
  0.0 316.1 jit_solution(14542344356930116117)
XLA Ops:
  7.2 0.0 copy-start
  7.2 0.0 all-reduce.5.cloned.1.call-start
  7.2 6.8 %convolution_bitcast_fusion = f32[2048,128]{1,0:T(8,128)} fusion(bf16[2,2048,1024]{2,1,0:T(8,128)(2,1)} %param.9, bf16[2,1024,128]{2,1,0:T(8,128)(2,1)} %param.10), kind=kOutput, calls=%fused_computation.1 | convolution fusion | flops 1073741824 | bytes 9961472 | tf_op jit(solution)/shard_map/trc,tck->rk/dot_general | solution.py:30
  14.1 0.0 all-reduce.5.cloned.1.call-update
  14.1 0.0 copy-start.3
  14.1 0.0 all-reduce.9.cloned.1.call-start
  14.1 0.0 copy-done
  14.1 0.0 copy-start.5
  14.2 6.1 %fusion.2 = f32[2,1024,256]{2,1,0:T(8,128)S(1)} fusion(bf16[2,2048,1024]{2,1,0:T(8,128)(2,1)} %param.9, bf16[256,2048]{1,0:T(8,128)(2,1)S(1)} %copy-done), kind=kOutput, calls=%fused_computation.7 | convolution fusion | flops 2147483648 | bytes 11534336 | tf_op jit(solution)/shard_map/sr,trc->tsc/dot_general | solution.py:33
  20.3 0.0 copy-done.3
  20.3 1.8 fusion
  22.1 0.0 copy-done.5
  22.2 6.6 %convolution_bitcast_fusion.2 = f32[1024,128]{1,0:T(8,128)} fusion(bf16[2,2048,1024]{2,1,0:T(8,128)(2,1)} %param.9, bf16[2,2048,128]{2,1,0:T(8,128)(2,1)S(1)} %copy-done.5), kind=kOutput, calls=%fused_computation.6 | convolution fusion | flops 1073741824 | bytes 9961472 | tf_op jit(solution)/shard_map/trc,trk->ck/dot_general | solution.py:26
  28.7 0.0 copy-start.4
  28.7 66.5 %all-reduce.5.cloned.1.call-done = f32[2048,128]{1,0:T(8,128)} async-done(((f32[2048,128]{1,0:T(8,128)}), f32[2048,128]{1,0:T(8,128)}) %all-reduce.5.cloned.1.call-update) | async-done | bytes 1048592 | tf_op jit(solution)/shard_map/psum | solution.py:41
  95.3 1.6 add.34
  96.9 2.4 fusion.13
  99.4 0.0 all-reduce.9.cloned.1.call-update
  99.4 0.0 all-reduce.7.cloned.1.call-start
  99.5 0.0 copy-done.4
  99.5 5.1 %convolution_bitcast_fusion.1 = f32[9,256,256]{2,0,1:T(8,128)} fusion(f32[2,256,256]{2,1,0:T(8,128)S(1)} %fusion, f32[9,2]{0,1:T(2,128)S(1)} %copy-done.4), kind=kOutput, calls=%fused_computation.3 | convolution fusion | flops 14155776 | bytes 2883656 | tf_op jit(solution)/shard_map/jt,tsu->jsu/dot_general | solution.py:37
  104.5 0.0 all-reduce.7.cloned.1.call-update
  104.6 0.2 reduce-scatter.2.cloned.1.call-start
  104.8 28.2 %all-reduce.9.cloned.1.call-done = (f32[128,128]{0,1:T(8,128)}, f32[1024,128]{1,0:T(8,128)}) async-done(((f32[128,128]{0,1:T(8,128)}, f32[1024,128]{1,0:T(8,128)}), (f32[128,128]{0,1:T(8,128)}, f32[1024,128]{1,0:T(8,128)})) %all-reduce.9.cloned.1.call-update) | async-done | bytes 589840 | tf_op jit(solution)/shard_map/psum | solution.py:42
  133.0 0.9 copy.14
  133.9 0.9 fusion.11
  134.8 11.7 %cholesky.16 = f32[128,128]{1,0:T(8,128)S(1)} custom-call(f32[128,128]{1,0:T(8,128)S(1)} %fusion.11), custom_call_target="Cholesky" | custom-call | tf_op jit(solution)/shard_map/jit(cholesky)/cholesky | solution.py:9
  146.5 0.6 compare_reduce_fusion
  147.2 0.7 fusion.9
  147.8 9.8 %custom-call.7 = f32[1,128,128]{1,2,0:T(8,128)S(1)} custom-call(f32[1,128,128]{2,1,0:T(8,128)S(1)} %fusion.9), custom_call_target="InvertDiagBlocksLowerTriangular" | custom-call | tf_op jit(solution)/shard_map/jit(_solve_triangular)/triangular_solve | solution.py:10
  157.7 1.0 convolution_multiply_fusion
  158.6 5.8 %fusion.5 = f32[128,2,1024]{2,0,1:T(8,128)} fusion(bf16[2,2048,1024]{2,1,0:T(8,128)(2,1)} %param.9, f32[2048,128]{1,0:T(8,128)S(1)} %convolution_multiply_fusion), kind=kOutput, calls=%fused_computation.10 | convolution fusion | flops 1074003968 | bytes 10485760 | tf_op jit(solution)/shard_map/rk,trc->ktc/dot_general | solution.py:44
  164.4 0.0 reduce-scatter.2.cloned.1.call-update
  164.4 116.8 %all-reduce.7.cloned.1.call-done = f32[9,256,256]{2,0,1:T(8,128)} async-done(((f32[9,256,256]{2,0,1:T(8,128)}), f32[9,256,256]{2,0,1:T(8,128)}) %all-reduce.7.cloned.1.call-update) | async-done | bytes 2359312 | tf_op jit(solution)/shard_map/psum | solution.py:38
  281.3 4.6 %copy_add_fusion = f32[9,256,256]{2,0,1:T(8,128)S(1)} fusion(f32[9,256,256]{2,0,1:T(8,128)} %all-reduce.7.cloned.1.call-done, f32[9,256,256]{2,1,0:T(8,128)} %param.16), kind=kLoop, calls=%fused_computation | loop fusion | flops 589824 | bytes 7077888 | tf_op jit(solution)/shard_map/add | solution.py:38
  285.8 0.0 copy-start.1
  285.8 0.0 copy-start.2
  285.8 2.8 copy.19
  288.6 0.0 copy-done.1
  288.6 0.0 copy-done.2
  288.6 0.8 add.37
  289.5 0.7 constant_dynamic-slice_fusion
  290.1 17.5 %reduce-scatter.2.cloned.1.call-done = f32[32,2,1024]{2,0,1:T(8,128)} async-done(((f32[128,2,1024]{2,0,1:T(8,128)}), f32[32,2,1024]{2,0,1:T(8,128)}) %reduce-scatter.2.cloned.1.call-update) | async-done | bytes 262160 | tf_op jit(solution)/shard_map/reduce_scatter | solution.py:51
  307.7 1.0 broadcast_multiply_fusion
  308.7 0.9 copy.18
  (1 shorter events, 0.0 us)
Async XLA Ops:
  7.2 7.0 %copy-start = (bf16[256,2048]{1,0:T(8,128)(2,1)S(1)}, bf16[256,2048]{1,0:T(8,128)(2,1)}, u32[]{:S(2)}) copy-start(bf16[256,2048]{1,0:T(8,128)(2,1)} %param.12) | copy-start | bytes 3145732
  7.2 88.1 %all-reduce.5.cloned.1.call-start = ((), (), s32[]{:S(2)}) async-start(), calls=%async_computation.1 | async-start | bytes 2097152 | tf_op jit(solution)/shard_map/psum | solution.py:41
  14.1 6.2 %copy-start.3 = (bf16[256,1024]{1,0:T(8,128)(2,1)S(1)}, bf16[256,1024]{1,0:T(8,128)(2,1)}, u32[]{:S(2)}) copy-start(bf16[256,1024]{1,0:T(8,128)(2,1)} %param.13) | copy-start | bytes 1572868
  14.1 118.9 %all-reduce.9.cloned.1.call-start = ((), (), s32[]{:S(2)}) async-start(), calls=%async_computation.4 | async-start | bytes 1179648 | tf_op jit(solution)/shard_map/psum | solution.py:42
  14.1 8.0 %copy-start.5 = (bf16[2,2048,128]{2,1,0:T(8,128)(2,1)S(1)}, bf16[2,2048,128]{2,1,0:T(8,128)(2,1)}, u32[]{:S(2)}) copy-start(bf16[2,2048,128]{2,1,0:T(8,128)(2,1)} %param.11) | copy-start | bytes 3145732
  28.7 70.7 %copy-start.4 = (f32[9,2]{0,1:T(2,128)S(1)}, f32[9,2]{0,1:T(2,128)}, u32[]{:S(2)}) copy-start(f32[9,2]{0,1:T(2,128)} %param.17) | copy-start | bytes 220
  99.4 181.9 %all-reduce.7.cloned.1.call-start = ((), (), s32[]{:S(2)}) async-start(), calls=%async_computation.3 | async-start | bytes 8388608 | tf_op jit(solution)/shard_map/psum | solution.py:38
  104.6 203.1 %reduce-scatter.2.cloned.1.call-start = ((), (), s32[]{:S(2)}) async-start(), calls=%async_computation.2 | async-start | bytes 1310720 | tf_op jit(solution)/shard_map/reduce_scatter | solution.py:51
  285.8 2.8 copy-start.1
  285.8 2.8 copy-start.2
Sparse Core Ops, SparseCore 0:
  14.2 81.0 all-reduce.4
  99.5 33.4 all-reduce.8
  138.5 142.6 all-reduce.6
  283.6 23.9 reduce-scatter.1
where the time goes:
time: 316 us
  waiting for transfers between devices  229 us (72%)
  matrix products  35.6 us (11%)
  other arithmetic  31.7 us (10%)
  between operations  13.9 us (4%)
  local copies, waits for them, and re-layouts  5.31 us (2%)
    psum x1, waiting for transfers between devices, body(): core = old_core + lax.psum(core_part, ('gx', 'gy'))  117 us
    psum x1, waiting for transfers between devices, body(): whole_rows = lax.psum(part_one, 'gy') + old_mode_one  66.5 us
    psum x1, waiting for transfers between devices, body(): lax.psum(jnp.dot(whole_rows.T, whole_rows, precision=lax.Precision.HIGHES...  28.2 us
    reduce_scatter x1, waiting for transfers between devices, body(): lax.psum_scatter(projected_part, 'gx', scatter_dimension=0, tiled=True)  17.5 us
    another operation x3, other arithmetic, orthonormal(): factor = jnp.linalg.cholesky(gram_matrix)  12.4 us
    another operation x2, other arithmetic, orthonormal(): jax.scipy.linalg.solve_triangular(factor, sketch_rows.T, lower=True)  10.5 us
    dot_general x1, matrix products, body(): jnp.einsum('trc,tck->rk', snapshots, mode_one_test, preferred_element_typ...  6.82 us
    dot_general x1, matrix products, body(): jnp.einsum('trc,trk->ck', snapshots, mode_two_test, preferred_element_typ...  6.59 us
  transfers between devices with their start and end apart: 4, of which 4 were waited for; matrix products, arithmetic and copies ran while one was open for 19% of the time, Pallas kernels for 0%

commit v1 on v0

--- a/solution.py
+++ b/solution.py
@@ -35,7 +35,7 @@
         "tsc,uc->tsu", folded, column_sketch.astype(jnp.float32), precision=lax.Precision.HIGHEST
     )
     core_part = jnp.einsum("jt,tsu->jsu", time_mix, core_part, precision=lax.Precision.HIGHEST)
-    core = old_core + lax.psum(core_part, ("gx", "gy"))
+    core = old_core + lax.psum(lax.psum(core_part, "gy"), "gx")
     row_share = tile_rows // lax.axis_size("gy")
     first_row = lax.axis_index("gy") * row_share
     whole_rows = lax.psum(part_one, "gy") + old_mode_one

time: 316 us -> 375 us (1.19)
  waiting for transfers between devices: 229 us -> 290 us
    psum x1 -> x0, waiting for transfers between devices: 117 us -> none  [body(): core = old_core + lax.psum(core_part, ('gx', 'gy'))]
    psum x1, waiting for transfers between devices: 66.5 us -> 180 us  [body(): whole_rows = lax.psum(part_one, 'gy') + old_mode_one]
    psum x1, waiting for transfers between devices: 28.2 us -> 94.2 us  [body(): lax.psum(jnp.dot(whole_rows.T, whole_rows, precision=lax.Precision.HIGHES...]
  transfers between devices with their start and end apart: 4 -> 3, of which waited for: 4 -> 3; matrix products, arithmetic and copies ran while one was open for 19% -> 4% of each run, Pallas kernels for 0% -> 0%
where the time goes in v1:
time: 375 us
  waiting for transfers between devices  290 us (77%)
  matrix products  32.1 us (9%)
  other arithmetic  31.4 us (8%)
  between operations  13.9 us (4%)
  local copies, waits for them, and re-layouts  6.48 us (2%)
    psum x1, waiting for transfers between devices, body(): whole_rows = lax.psum(part_one, 'gy') + old_mode_one  180 us
    psum x1, waiting for transfers between devices, body(): lax.psum(jnp.dot(whole_rows.T, whole_rows, precision=lax.Precision.HIGHES...  94.2 us
    reduce_scatter x1, waiting for transfers between devices, body(): lax.psum_scatter(projected_part, 'gx', scatter_dimension=0, tiled=True)  16.2 us
    another operation x3, other arithmetic, orthonormal(): factor = jnp.linalg.cholesky(gram_matrix)  12.4 us
    another operation x2, other arithmetic, orthonormal(): jax.scipy.linalg.solve_triangular(factor, sketch_rows.T, lower=True)  10.5 us
  transfers between devices with their start and end apart: 3, of which 3 were waited for; matrix products, arithmetic and copies ran while one was open for 4% of the time, Pallas kernels for 0%

profile of v1, /device:TPU:0, one launch (start us, length us, event | category | flops | bytes accessed | tf_op | source)
XLA Modules:
  0.0 374.6 jit_solution(10225474328841491327)
XLA Ops:
  7.2 0.0 copy-start
  7.2 0.0 copy-start.8
  7.2 0.0 all-reduce.5.cloned.1.call-start
  7.2 1.2 copy-done
  8.4 0.0 copy-start.1
  8.4 6.2 %fusion.2 = f32[2,1024,256]{2,1,0:T(8,128)S(1)} fusion(bf16[2,2048,1024]{2,1,0:T(8,128)(2,1)} %param.9, bf16[256,2048]{1,0:T(8,128)(2,1)S(1)} %copy-done), kind=kOutput, calls=%fused_computation.7 | convolution fusion | flops 2147483648 | bytes 11534336 | tf_op jit(solution)/shard_map/sr,trc->tsc/dot_general | solution.py:33
  14.6 0.0 copy-done.8
  14.6 0.0 copy-done.1
  14.6 0.0 copy-start.5
  14.6 0.0 copy-start.6
  14.6 3.4 convolution_bitcast_fusion
  18.0 0.0 copy-done.5
  18.0 1.8 fusion
  19.9 0.0 copy-done.6
  19.9 0.0 copy-start.7
  19.9 5.1 %convolution_bitcast_fusion.1 = f32[9,256,256]{2,0,1:T(8,128)} fusion(f32[2,256,256]{2,1,0:T(8,128)S(1)} %fusion, f32[9,2]{0,1:T(2,128)S(1)} %copy-done.6), kind=kOutput, calls=%fused_computation.3 | convolution fusion | flops 14155776 | bytes 2883656 | tf_op jit(solution)/shard_map/jt,tsu->jsu/dot_general | solution.py:37
  25.0 0.0 all-reduce.5.cloned.1.call-update
  25.0 0.0 copy-start.2
  25.0 0.2 all-reduce.7.cloned.1.call-start
  25.2 0.0 copy-done.7
  25.2 6.6 %convolution_bitcast_fusion.2 = f32[1024,128]{1,0:T(8,128)} fusion(bf16[2,2048,1024]{2,1,0:T(8,128)(2,1)} %param.9, bf16[2,2048,128]{2,1,0:T(8,128)(2,1)S(1)} %copy-done.7), kind=kOutput, calls=%fused_computation.6 | convolution fusion | flops 1073741824 | bytes 9961472 | tf_op jit(solution)/shard_map/trc,trk->ck/dot_general | solution.py:26
  31.8 179.8 %all-reduce.5.cloned.1.call-done = (f32[2048,128]{1,0:T(8,128)}, f32[9,256,256]{2,0,1:T(8,128)}) async-done(((f32[2048,128]{1,0:T(8,128)}, f32[9,256,256]{2,0,1:T(8,128)}), (f32[2048,128]{1,0:T(8,128)}, f32[9,256,256]{2,0,1:T(8,128)})) %all-reduce.5.cloned.1.call-update) | async-done | bytes 3407888 | tf_op jit(solution)/shard_map/psum | solution.py:41
  211.6 0.0 copy-done.2
  211.6 1.3 add.36
  213.0 2.4 fusion.13
  215.4 0.0 all-reduce.7.cloned.1.call-update
  215.5 0.0 reduce-scatter.2.cloned.1.call-start
  215.5 94.2 %all-reduce.7.cloned.1.call-done = (f32[128,128]{0,1:T(8,128)}, f32[1024,128]{1,0:T(8,128)}, f32[9,256,256]{2,0,1:T(8,128)}) async-done(((f32[128,128]{0,1:T(8,128)}, f32[1024,128]{1,0:T(8,128)}, f32[9,256,256]{2,0,1:T(8,128)}), (f32[128,128]{0,1:T(8,128)}, f32[1024,128]{1,0:T(8,128)}, f32[9,256,256]{2,0,1:T(8,128)})) %all-reduce.7.cloned.1.call-update) | async-done | bytes 2949136 | tf_op jit(solution)/shard_map/psum | solution.py:42
  309.7 0.9 copy.14
  310.7 0.9 fusion.11
  311.5 11.7 %cholesky.16 = f32[128,128]{1,0:T(8,128)S(1)} custom-call(f32[128,128]{1,0:T(8,128)S(1)} %fusion.11), custom_call_target="Cholesky" | custom-call | tf_op jit(solution)/shard_map/jit(cholesky)/cholesky | solution.py:9
  323.3 0.6 compare_reduce_fusion
  323.9 0.7 fusion.9
  324.6 9.8 %custom-call.7 = f32[1,128,128]{1,2,0:T(8,128)S(1)} custom-call(f32[1,128,128]{2,1,0:T(8,128)S(1)} %fusion.9), custom_call_target="InvertDiagBlocksLowerTriangular" | custom-call | tf_op jit(solution)/shard_map/jit(_solve_triangular)/triangular_solve | solution.py:10
  334.4 1.0 convolution_multiply_fusion
  335.4 5.6 %fusion.5 = f32[128,2,1024]{2,0,1:T(8,128)} fusion(bf16[2,2048,1024]{2,1,0:T(8,128)(2,1)} %param.9, f32[2048,128]{1,0:T(8,128)S(1)} %convolution_multiply_fusion), kind=kOutput, calls=%fused_computation.10 | convolution fusion | flops 1074003968 | bytes 10485760 | tf_op jit(solution)/shard_map/rk,trc->ktc/dot_general | solution.py:44
  341.0 0.0 reduce-scatter.2.cloned.1.call-update
  341.0 4.6 %copy_add_fusion = f32[9,256,256]{2,0,1:T(8,128)S(1)} fusion(f32[9,256,256]{2,0,1:T(8,128)} %get-tuple-element.12, f32[9,256,256]{2,1,0:T(8,128)} %param.16), kind=kLoop, calls=%fused_computation | loop fusion | flops 589824 | bytes 7077888 | tf_op jit(solution)/shard_map/add | solution.py:38
  345.6 0.0 copy-start.3
  345.6 0.0 copy-start.4
  345.6 2.8 copy.19
  348.4 0.0 copy-done.3
  348.4 0.0 copy-done.4
  348.4 0.8 add.39
  349.2 0.7 constant_dynamic-slice_fusion
  349.9 16.2 %reduce-scatter.2.cloned.1.call-done = f32[32,2,1024]{2,0,1:T(8,128)} async-done(((f32[128,2,1024]{2,0,1:T(8,128)}), f32[32,2,1024]{2,0,1:T(8,128)}) %reduce-scatter.2.cloned.1.call-update) | async-done | bytes 262160 | tf_op jit(solution)/shard_map/reduce_scatter | solution.py:51
  366.1 1.0 broadcast_multiply_fusion
  367.1 0.9 copy.18
  (1 shorter events, 0.0 us)
Async XLA Ops:
  7.2 1.2 copy-start
  7.2 7.4 %copy-start.8 = (bf16[2,1024,128]{2,1,0:T(8,128)(2,1)S(1)}, bf16[2,1024,128]{2,1,0:T(8,128)(2,1)}, u32[]{:S(2)}) copy-start(bf16[2,1024,128]{2,1,0:T(8,128)(2,1)} %param.10) | copy-start | bytes 1572868
  7.2 204.4 %all-reduce.5.cloned.1.call-start = ((), (), s32[]{:S(2)}) async-start(), calls=%async_computation.2 | async-start | bytes 10485760 | tf_op jit(solution)/shard_map/psum | solution.py:41
  8.4 6.2 %copy-start.1 = (bf16[2,2048,1024]{2,1,0:T(8,128)(2,1)S(1)}, bf16[2,2048,1024]{2,1,0:T(8,128)(2,1)}, u32[]{:S(2)}) copy-start(bf16[2,2048,1024]{2,1,0:T(8,128)(2,1)} %param.9) | copy-start | bytes 25165828
  14.6 3.4 copy-start.5
  14.6 5.2 %copy-start.6 = (f32[9,2]{0,1:T(2,128)S(1)}, f32[9,2]{0,1:T(2,128)}, u32[]{:S(2)}) copy-start(f32[9,2]{0,1:T(2,128)} %param.17) | copy-start | bytes 220
  19.9 5.4 %copy-start.7 = (bf16[2,2048,128]{2,1,0:T(8,128)(2,1)S(1)}, bf16[2,2048,128]{2,1,0:T(8,128)(2,1)}, u32[]{:S(2)}) copy-start(bf16[2,2048,128]{2,1,0:T(8,128)(2,1)} %param.11) | copy-start | bytes 3145732
  25.0 186.7 %copy-start.2 = (f32[2048,128]{1,0:T(8,128)S(1)}, f32[2048,128]{1,0:T(8,128)}, u32[]{:S(2)}) copy-start(f32[2048,128]{1,0:T(8,128)} %param.14) | copy-start | bytes 3145732
  25.0 284.7 %all-reduce.7.cloned.1.call-start = ((), (), s32[]{:S(2)}) async-start(), calls=%async_computation.3 | async-start | bytes 9568256 | tf_op jit(solution)/shard_map/psum | solution.py:42
  215.5 150.7 %reduce-scatter.2.cloned.1.call-start = ((), (), s32[]{:S(2)}) async-start(), calls=%async_computation.1 | async-start | bytes 1310720 | tf_op jit(solution)/shard_map/reduce_scatter | solution.py:51
  345.6 2.8 copy-start.3
  345.6 2.8 copy-start.4
Sparse Core Ops, SparseCore 0:
  25.1 186.4 all-reduce.4
  215.6 94.1 all-reduce.6
  341.1 24.9 reduce-scatter.1
